TPU v7x, 512 devices: a whole 4x4x16 slice. The times are simulated.
512 devices in a mesh: rows: 128 (over x, z, core), rep: 4 (over y).
Axes of the slice: x: 4, y: 4, z: 16, core: 2. Of those that a mesh axis runs over, the one named last changes fastest.
Arguments:
- feats: bfloat16 [4, 32768, 512], P('rep', 'rows'), may hold values from -24 to 24
- grad_out: bfloat16 [4, 32768, 512], P('rep', 'rows'), may hold values from -6 to 6
- qkv_weight: bfloat16 [512, 1536], P('rows'), may hold values from -0.25 to 0.25
- proj_weight: bfloat16 [512, 512], P('rows'), may hold values from -0.25 to 0.25
- to_hilbert: int32 [4, 16384], P('rep', 'rows'), may hold values from 0 to 16383, as said below
- to_zorder: int32 [4, 16384], P('rep', 'rows'), may hold values from 0 to 16383, as said below
Outputs:
- grad_feats: bfloat16 [4, 32768, 512], P('rep', 'rows')
- qkv_grad: float32 [512, 1536], P('rows')
- proj_grad: float32 [512, 512], P('rows')
Inputs may be any that keep to these rules, and one draw needn't show every extreme that they name: to_hilbert[s] is a permutation of the blocks of scene s and to_zorder[s] its inverse; of the 128 Z-order blocks of one device, at most 2 have Hilbert positions on any one device, and exactly 2 for some pair of devices in every scene. `to_zorder`: the inverse of to_hilbert in every scene.
All inputs are finite; a program needn't handle non-finite values.
Results may differ from a plain program's by a relative error of at most 0.015.
The roundings to bfloat16 on the way count: a program that leaves them out, or rounds other values in their place, can miss the bound.
Values may be sent and summed in bfloat16 or wider, within the bound.
No kernel may reach another device: no remote copies, remote signals or barrier semaphores. Data moves between devices by JAX's collectives and lax.ppermute only.
A program may use at most 64 MiB of HBM per device.

v0:
```python
import jax
import jax.numpy as jnp
from jax import lax
from jax.sharding import PartitionSpec as P

HEADS = 8
CAP = 2


def from_partner(block, axis, apart):
    count = lax.axis_size(axis)
    route = []
    for low in range(count):
        high = low | 1 << apart
        if high != low and high < count:
            route += [(low, high), (high, low)]
    return lax.ppermute(block, axis, route)


def move_blocks(outgoing):
    return lax.all_to_all(outgoing, "rows", split_axis=0, concat_axis=0, tiled=True)


def rank_within(order_keys, owners):
    same_owner = owners[None, :] == owners[:, None]
    earlier = order_keys[None, :] < order_keys[:, None]
    return jnp.sum(jnp.logical_and(same_owner, earlier).astype(jnp.int32), axis=1)


def contract_rows(left, right):
    return lax.dot_general(
        left, right, (((0,), (0,)), ((), ())), preferred_element_type=jnp.float32
    )


def contract_cols(left, right):
    return lax.dot_general(
        left, right, (((1,), (1,)), ((), ())), preferred_element_type=jnp.float32
    )


def per_device(feats, grad_out, qkv_weight, proj_weight, to_hilbert, to_zorder):
    peer_count = lax.axis_size("rows")
    feature = feats[0]
    rows_dev, channels = feature.shape
    head_size = channels // HEADS
    scale = head_size ** (-0.5)
    blocks_dev = to_hilbert.shape[1]
    slot_count = peer_count * CAP
    w_qkv, w_proj = (
        lax.all_gather(qkv_weight, "rows", axis=0, tiled=True),
        lax.all_gather(proj_weight, "rows", axis=0, tiled=True),
    )
    forward_list = to_hilbert[0]
    inverse_list = to_zorder[0]
    local_ids = jnp.arange(blocks_dev, dtype=jnp.int32)
    slot_ids = jnp.arange(slot_count, dtype=jnp.int32)
    target_dev = forward_list // blocks_dev
    send_slot = target_dev * CAP + rank_within(local_ids, target_dev)
    send_table = (send_slot[None, :] == slot_ids[:, None]).astype(jnp.bfloat16)
    source_dev = inverse_list // blocks_dev
    recv_slot = source_dev * CAP + rank_within(inverse_list, source_dev)
    recv_table = (recv_slot[:, None] == slot_ids[None, :]).astype(jnp.bfloat16)
    zblocks = grad_out[0].reshape(blocks_dev, -1)
    outgoing = jnp.dot(send_table, zblocks, preferred_element_type=jnp.float32).astype(jnp.bfloat16)
    arrived = move_blocks(outgoing.reshape(peer_count, CAP, -1)).reshape(slot_count, -1)
    grad_hil = jnp.dot(recv_table, arrived, preferred_element_type=jnp.float32).astype(jnp.bfloat16)
    grad_hil = grad_hil.reshape(rows_dev, channels)
    qkv = jnp.dot(feature, w_qkv, preferred_element_type=jnp.float32).astype(jnp.bfloat16)
    query = qkv[:, :channels]
    keyval = qkv[:, channels:]
    grad_attn = contract_cols(grad_hil, w_proj).astype(jnp.bfloat16)
    other_kv = from_partner(keyval, "rows", 0)
    keys_all = jnp.concatenate([keyval[:, :channels], other_kv[:, :channels]], axis=0)
    values_all = jnp.concatenate([keyval[:, channels:], other_kv[:, channels:]], axis=0)
    attn_parts, dq_parts, dk_parts, dv_parts = ([], [], [], [])
    for head_index in range(HEADS):
        lo_col = head_index * head_size
        q_head = query[:, lo_col : lo_col + head_size]
        k_head = keys_all[:, lo_col : lo_col + head_size]
        v_head = values_all[:, lo_col : lo_col + head_size]
        g_head = grad_attn[:, lo_col : lo_col + head_size]
        score = contract_cols(q_head, k_head) * scale
        row_max = jnp.max(score, axis=1, keepdims=True)
        raised = jnp.exp(score - row_max)
        row_sum = jnp.sum(raised, axis=1, keepdims=True)
        probs = raised / row_sum
        probs_b = probs.astype(jnp.bfloat16)
        attn_parts.append(
            jnp.dot(probs_b, v_head, preferred_element_type=jnp.float32).astype(jnp.bfloat16)
        )
        dprob = contract_cols(g_head, v_head)
        delta = jnp.sum(probs * dprob, axis=1, keepdims=True)
        dscore = (probs * (dprob - delta) * scale).astype(jnp.bfloat16)
        dq_parts.append(jnp.dot(dscore, k_head, preferred_element_type=jnp.float32))
        dk_parts.append(contract_rows(dscore, q_head))
        dv_parts.append(contract_rows(probs_b, g_head))
    grad_q = jnp.concatenate(dq_parts, axis=1)
    grad_k = jnp.concatenate(dk_parts, axis=1)
    grad_v = jnp.concatenate(dv_parts, axis=1)
    other_k, other_v = (
        from_partner(grad_k[rows_dev:].astype(jnp.bfloat16), "rows", 0).astype(jnp.float32),
        from_partner(grad_v[rows_dev:].astype(jnp.bfloat16), "rows", 0).astype(jnp.float32),
    )
    grad_k = grad_k[:rows_dev] + other_k
    grad_v = grad_v[:rows_dev] + other_v
    grad_qkv = jnp.concatenate([grad_q, grad_k, grad_v], axis=1).astype(jnp.bfloat16)
    attn = jnp.concatenate(attn_parts, axis=1)
    grad_hfeat = contract_cols(grad_qkv, w_qkv).astype(jnp.bfloat16)
    hblocks = grad_hfeat.reshape(blocks_dev, -1)
    going_back = contract_rows(recv_table, hblocks).astype(jnp.bfloat16)
    returned = move_blocks(going_back.reshape(peer_count, CAP, -1)).reshape(slot_count, -1)
    grad_z = contract_rows(send_table, returned).astype(jnp.bfloat16).reshape(rows_dev, channels)
    share = channels // peer_count
    term = jnp.concatenate(
        [contract_rows(feature, grad_qkv), contract_rows(attn, grad_hil)], axis=1
    )
    total = lax.psum(term, ("rows", "rep"))
    owned = lax.dynamic_slice_in_dim(total, lax.axis_index("rows") * share, share, 0)
    return (grad_z[None], owned[:, : 3 * channels], owned[:, 3 * channels :])


def solution(mesh):
    placed = (
        P("rep", "rows", None),
        P("rep", "rows", None),
        P("rows", None),
        P("rows", None),
        P("rep", "rows"),
        P("rep", "rows"),
    )
    return jax.shard_map(
        per_device,
        mesh=mesh,
        in_specs=placed,
        out_specs=(P("rep", "rows", None), P("rows", None), P("rows", None)),
        check_vma=False,
    )
```

profile of v0, /device:TPU:2, one launch (start us, length us, event | category | flops | bytes accessed | tf_op | source)
XLA Modules:
  0.0 721.0 jit_solution(14029525855574183305)
XLA Ops:
  7.2 0.7 all-gather.4.cloned.1.call-update
  7.9 1.0 reshape_squeeze.3
  9.0 0.7 and_select_fusion.2
  10.5 0.7 fusion.113
  11.5 1.0 reshape.119
  12.5 19.5 %all-to-all-start = ((bf16[128,2,1024]{2,1,0:T(2,128)(2,1)}), bf16[128,2,1024]{2,1,0:T(2,128)(2,1)S(1)}, u32[]{:S(2)}, u32[]{:S(2)}) async-start(bf16[128,2,1024]{2,1,0:T(2,128)(2,1)} %reshape.119), calls=%async_computation | async-start | bytes 1048576 | tf_op jit(solution)/shard_map/all_to_all | solution.py:21
  32.0 100.5 %all-gather.1 = bf16[128,4,512]{2,1,0:T(4,128)(2,1)S(1)} all-gather(bf16[1,4,512]{2,1,0:T(4,128)(2,1)S(1)} %bitcast.64), channel_id=1, replica_groups=mesh['rows'=128,'rep'=4] {'rows'}, dimensions={0}, use_global_device_ids=true | all-gather | bytes 528384 | tf_op jit(solution)/shard_map/all_gather | solution.py:52
  132.9 1.0 reshape.120
  133.9 22.9 %all-gather.4.cloned.1.call-done = bf16[128,4,1536]{2,1,0:T(4,128)(2,1)} async-done(((bf16[1,4,1536]{2,1,0:T(4,128)(2,1)}), bf16[128,4,1536]{2,1,0:T(4,128)(2,1)}) %all-gather.4.cloned.1.call-update) | async-done | bytes 1572880 | tf_op jit(solution)/shard_map/all_gather | solution.py:51
  156.9 2.7 reshape.126
  160.2 0.9 slice.187
  161.0 2.3 collective-permute-start
  163.4 1.0 convolution_convert_fusion.6
  164.4 1.0 reshape.121
  165.8 1.1 fusion.160
  180.5 2.1 collective-permute-start.2
  182.6 1.3 fusion.169
  188.6 2.4 collective-permute-start.1
  192.2 1.3 convolution_convert_fusion.4
  194.1 1.7 reshape.122
  195.8 2.2 convolution_convert_fusion.1
  198.0 2.1 reshape.123
  200.1 12.8 %all-to-all-start.1 = ((bf16[128,2,1024]{2,1,0:T(2,128)(2,1)}), bf16[128,2,1024]{2,1,0:T(2,128)(2,1)}, u32[]{:S(2)}, u32[]{:S(2)}) async-start(bf16[128,2,1024]{2,1,0:T(2,128)(2,1)} %reshape.123), calls=%async_computation.1 | async-start | bytes 1048576 | tf_op jit(solution)/shard_map/all_to_all | solution.py:21
  212.9 3.6 pad_maximum_fusion
  216.5 29.6 %all-to-all-done.1 = bf16[128,2,1024]{2,1,0:T(2,128)(2,1)} async-done(((bf16[128,2,1024]{2,1,0:T(2,128)(2,1)}), bf16[128,2,1024]{2,1,0:T(2,128)(2,1)}, u32[]{:S(2)}, u32[]{:S(2)}) %all-to-all-start.1) | async-done | bytes 524320 | tf_op jit(solution)/shard_map/all_to_all | solution.py:21
  246.2 1.2 reshape.124
  247.7 0.8 broadcast_in_dim_reshape.3
  248.5 461.6 %all-reduce.2.cloned.1.call-done = f32[512,2048]{0,1:T(8,128)} async-done(((f32[512,2048]{0,1:T(8,128)}), f32[512,2048]{0,1:T(8,128)}) %all-reduce.2.cloned.1.call-update) | async-done | bytes 4194320 | tf_op jit(solution)/shard_map/psum | solution.py:118
  710.0 1.4 constant_dynamic-slice_fusion
  711.4 0.9 copy.13
  712.3 1.1 dynamic-slice.1
  713.4 0.7 copy.14
  (98 shorter events, 22.6 us)
Async XLA Ops:
  7.2 152.4 %copy-start = (bf16[1,256,512]{2,1,0:T(8,128)(2,1)S(1)}, bf16[1,256,512]{2,1,0:T(8,128)(2,1)}, u32[]{:S(2)}) copy-start(bf16[1,256,512]{2,1,0:T(8,128)(2,1)} %param.6) | copy-start | bytes 786436
  7.2 24.8 %copy-start.2 = (bf16[4,512]{1,0:T(4,128)(2,1)S(1)}, bf16[4,512]{1,0:T(4,128)(2,1)}, u32[]{:S(2)}) copy-start(bf16[4,512]{1,0:T(4,128)(2,1)} %param.9) | copy-start | bytes 12292
  7.2 125.5 %copy-start.3 = (s32[1,128]{1,0:T(1,128)S(1)}, s32[1,128]{1,0:T(1,128)}, u32[]{:S(2)}) copy-start(s32[1,128]{1,0:T(1,128)} %param.11) | copy-start | bytes 1540
  7.2 149.7 %all-gather.4.cloned.1.call-start = ((), (), s32[]{:S(2)}) async-start(), calls=%async_computation.3 | async-start | bytes 1585152 | tf_op jit(solution)/shard_map/all_gather | solution.py:51
  12.5 120.5 %all-to-all-start = ((bf16[128,2,1024]{2,1,0:T(2,128)(2,1)}), bf16[128,2,1024]{2,1,0:T(2,128)(2,1)S(1)}, u32[]{:S(2)}, u32[]{:S(2)}) async-start(bf16[128,2,1024]{2,1,0:T(2,128)(2,1)} %reshape.119), calls=%async_computation | async-start | bytes 1048576 | tf_op jit(solution)/shard_map/all_to_all | solution.py:21
  159.6 3.8 copy-start.1
  161.0 4.8 collective-permute-start
  180.5 11.7 %collective-permute-start.2 = (bf16[256,512]{0,1:T(8,128)(2,1)S(1)}, bf16[256,512]{0,1:T(8,128)(2,1)S(1)}, u32[]{:S(2)}, u32[]{:S(2)}) collective-permute-start(bf16[256,512]{0,1:T(8,128)(2,1)S(1)} %slice.454), channel_id=1, source_target_pairs={{0,4},{4,0},{8,12},{12,8},{16,20},{20,16},{24,28},{28,24},{32,36},... | collective-permute-start | bytes 786440 | tf_op jit(solution)/shard_map/ppermute | solution.py:17
  188.6 3.4 collective-permute-start.1
  200.1 46.1 %all-to-all-start.1 = ((bf16[128,2,1024]{2,1,0:T(2,128)(2,1)}), bf16[128,2,1024]{2,1,0:T(2,128)(2,1)}, u32[]{:S(2)}, u32[]{:S(2)}) async-start(bf16[128,2,1024]{2,1,0:T(2,128)(2,1)} %reshape.123), calls=%async_computation.1 | async-start | bytes 1048576 | tf_op jit(solution)/shard_map/all_to_all | solution.py:21
  212.9 497.2 %all-reduce.2.cloned.1.call-start = ((), (), s32[]{:S(2)}) async-start(), calls=%async_computation.2 | async-start | bytes 8388608 | tf_op jit(solution)/shard_map/psum | solution.py:118
Sparse Core Ops, SparseCore 0:
  11.1 145.7 all-gather.3
  219.2 490.8 all-reduce.1
where the time goes:
time: 722 us; the launch traced here: 721 us
  waiting for transfers between devices  515 us (71%)
  blocking collectives  101 us (14%)
  starting transfers between devices  39.3 us (5%)
  matrix products  22.5 us (3%)
  local copies, waits for them, and re-layouts  18.9 us (3%)
  between operations  14.4 us (2%)
  other arithmetic  9.94 us (1%)
    psum x1, waiting for transfers between devices, per_device(): total = lax.psum(term, ('rows', 'rep'))  462 us
    all_gather x1, blocking collectives, per_device(): lax.all_gather(proj_weight, 'rows', axis=0, tiled=True)  101 us
    all_to_all x2, starting transfers between devices, move_blocks(): lax.all_to_all(outgoing, 'rows', split_axis=0, concat_axis=0, tiled=True)  32.3 us
    all_to_all x2, waiting for transfers between devices, move_blocks(): lax.all_to_all(outgoing, 'rows', split_axis=0, concat_axis=0, tiled=True)  29.6 us
    all_gather x1, waiting for transfers between devices, per_device(): lax.all_gather(qkv_weight, 'rows', axis=0, tiled=True)  22.9 us
  transfers between devices with their start and end apart: 7, of which 4 were waited for; matrix products, arithmetic and copies ran while one was open for 3% of the time, Pallas kernels for 0%

commit v1 on v0

--- a/solution.py
+++ b/solution.py
@@ -115,7 +115,8 @@
     term = jnp.concatenate(
         [contract_rows(feature, grad_qkv), contract_rows(attn, grad_hil)], axis=1
     )
-    total = lax.psum(term, ("rows", "rep"))
+    half = lax.psum(term, "rows")
+    total = lax.psum(half, "rep")
     owned = lax.dynamic_slice_in_dim(total, lax.axis_index("rows") * share, share, 0)
     return (grad_z[None], owned[:, : 3 * channels], owned[:, 3 * channels :])
 

time: 722 us -> 672 us (0.931)
  the two profiles are of different devices: /device:TPU:2 before, /device:TPU:1 now
where the time goes in v1:
time: 672 us; the launch traced here: 671 us
  waiting for transfers between devices  470 us (70%)
  blocking collectives  101 us (15%)
  starting transfers between devices  42.4 us (6%)
  matrix products  19 us (3%)
  local copies, waits for them, and re-layouts  16.1 us (2%)
  between operations  14.2 us (2%)
  other arithmetic  8.76 us (1%)
    psum x1, waiting for transfers between devices, per_device(): half = lax.psum(term, 'rows')  353 us
    all_gather x1, blocking collectives, per_device(): lax.all_gather(proj_weight, 'rows', axis=0, tiled=True)  101 us
    psum x1, waiting for transfers between devices, per_device(): total = lax.psum(half, 'rep')  58.8 us
    all_to_all x2, starting transfers between devices, move_blocks(): lax.all_to_all(outgoing, 'rows', split_axis=0, concat_axis=0, tiled=True)  35.4 us
    all_to_all x2, waiting for transfers between devices, move_blocks(): lax.all_to_all(outgoing, 'rows', split_axis=0, concat_axis=0, tiled=True)  33.2 us
    all_gather x1, waiting for transfers between devices, per_device(): lax.all_gather(qkv_weight, 'rows', axis=0, tiled=True)  23.7 us
  transfers between devices with their start and end apart: 8, of which 5 were waited for; matrix products, arithmetic and copies ran while one was open for 3% of the time, Pallas kernels for 0%

profile of v1, /device:TPU:1, one launch (start us, length us, event | category | flops | bytes accessed | tf_op | source)
XLA Modules:
  0.0 671.2 jit_solution(14868801363304208827)
XLA Ops:
  7.2 0.7 all-gather.4.cloned.1.call-update
  7.9 1.0 reshape_squeeze.3
  9.0 0.7 and_select_fusion.2
  9.6 0.7 fusion.202
  10.5 0.7 fusion.113
  11.5 1.0 reshape.119
  12.5 20.4 %all-to-all-start = ((bf16[128,2,1024]{2,1,0:T(2,128)(2,1)}), bf16[128,2,1024]{2,1,0:T(2,128)(2,1)S(1)}, u32[]{:S(2)}, u32[]{:S(2)}) async-start(bf16[128,2,1024]{2,1,0:T(2,128)(2,1)} %reshape.119), calls=%async_computation | async-start | bytes 1048576 | tf_op jit(solution)/shard_map/all_to_all | solution.py:21
  32.9 101.0 %all-gather.1 = bf16[128,4,512]{2,1,0:T(4,128)(2,1)S(1)} all-gather(bf16[1,4,512]{2,1,0:T(4,128)(2,1)S(1)} %bitcast.64), channel_id=1, replica_groups=mesh['rows'=128,'rep'=4] {'rows'}, dimensions={0}, use_global_device_ids=true | all-gather | bytes 528384 | tf_op jit(solution)/shard_map/all_gather | solution.py:52
  134.4 1.0 reshape.120
  135.4 23.7 %all-gather.4.cloned.1.call-done = bf16[128,4,1536]{2,1,0:T(4,128)(2,1)} async-done(((bf16[1,4,1536]{2,1,0:T(4,128)(2,1)}), bf16[128,4,1536]{2,1,0:T(4,128)(2,1)}) %all-gather.4.cloned.1.call-update) | async-done | bytes 1572880 | tf_op jit(solution)/shard_map/all_gather | solution.py:51
  159.1 2.7 reshape.126
  162.5 0.9 slice.187
  163.3 2.3 collective-permute-start
  165.7 1.0 convolution_convert_fusion.6
  166.6 1.0 reshape.121
  168.1 1.1 fusion.160
  182.7 2.2 collective-permute-start.2
  189.9 2.4 collective-permute-start.1
  192.7 0.6 collective-permute-done.1
  193.5 0.9 copy-done.2
  195.0 2.4 pad_maximum_fusion
  197.5 352.6 %all-reduce.3.cloned.1.call-done = f32[512,2048]{0,1:T(8,128)} async-done(((f32[512,2048]{0,1:T(8,128)}), f32[512,2048]{0,1:T(8,128)}) %all-reduce.3.cloned.1.call-update) | async-done | bytes 4194320 | tf_op jit(solution)/shard_map/psum | solution.py:118
  550.1 0.6 convolution_convert_fusion.4
  551.3 1.0 reshape.123
  552.3 15.0 %all-to-all-start.1 = ((bf16[128,2,1024]{2,1,0:T(2,128)(2,1)}), bf16[128,2,1024]{2,1,0:T(2,128)(2,1)S(1)}, u32[]{:S(2)}, u32[]{:S(2)}) async-start(bf16[128,2,1024]{2,1,0:T(2,128)(2,1)} %reshape.123), calls=%async_computation.1 | async-start | bytes 1048576 | tf_op jit(solution)/shard_map/all_to_all | solution.py:21
  567.3 33.2 %all-to-all-done.1 = bf16[128,2,1024]{2,1,0:T(2,128)(2,1)S(1)} async-done(((bf16[128,2,1024]{2,1,0:T(2,128)(2,1)}), bf16[128,2,1024]{2,1,0:T(2,128)(2,1)S(1)}, u32[]{:S(2)}, u32[]{:S(2)}) %all-to-all-start.1) | async-done | bytes 524320 | tf_op jit(solution)/shard_map/all_to_all | solution.py:21
  601.0 0.8 broadcast_in_dim_reshape.3
  601.8 58.8 %all-reduce.5.cloned.1.call-done = f32[512,2048]{0,1:T(8,128)} async-done(((f32[512,2048]{0,1:T(8,128)}), f32[512,2048]{0,1:T(8,128)}) %all-reduce.5.cloned.1.call-update) | async-done | bytes 4194320 | tf_op jit(solution)/shard_map/psum | solution.py:119
  660.6 1.4 constant_dynamic-slice_fusion
  662.0 0.9 copy.13
  662.8 1.1 dynamic-slice.1
  663.9 0.7 copy.14
  (105 shorter events, 22.5 us)
Async XLA Ops:
  7.2 154.7 %copy-start = (bf16[1,256,512]{2,1,0:T(8,128)(2,1)S(1)}, bf16[1,256,512]{2,1,0:T(8,128)(2,1)}, u32[]{:S(2)}) copy-start(bf16[1,256,512]{2,1,0:T(8,128)(2,1)} %param.6) | copy-start | bytes 786436
  7.2 25.7 %copy-start.4 = (bf16[4,512]{1,0:T(4,128)(2,1)S(1)}, bf16[4,512]{1,0:T(4,128)(2,1)}, u32[]{:S(2)}) copy-start(bf16[4,512]{1,0:T(4,128)(2,1)} %param.9) | copy-start | bytes 12292
  7.2 126.9 %copy-start.5 = (s32[1,128]{1,0:T(1,128)S(1)}, s32[1,128]{1,0:T(1,128)}, u32[]{:S(2)}) copy-start(s32[1,128]{1,0:T(1,128)} %param.11) | copy-start | bytes 1540
  7.2 151.9 %all-gather.4.cloned.1.call-start = ((), (), s32[]{:S(2)}) async-start(), calls=%async_computation.4 | async-start | bytes 1585152 | tf_op jit(solution)/shard_map/all_gather | solution.py:51
  12.5 121.9 %all-to-all-start = ((bf16[128,2,1024]{2,1,0:T(2,128)(2,1)}), bf16[128,2,1024]{2,1,0:T(2,128)(2,1)S(1)}, u32[]{:S(2)}, u32[]{:S(2)}) async-start(bf16[128,2,1024]{2,1,0:T(2,128)(2,1)} %reshape.119), calls=%async_computation | async-start | bytes 1048576 | tf_op jit(solution)/shard_map/all_to_all | solution.py:21
  32.9 517.2 %all-reduce.3.cloned.1.call-start = ((), (), s32[]{:S(2)}) async-start(), calls=%async_computation.2 | async-start | bytes 8388608 | tf_op jit(solution)/shard_map/psum | solution.py:118
  161.9 3.8 copy-start.1
  163.3 4.7 collective-permute-start
  182.7 10.7 %collective-permute-start.2 = (bf16[256,512]{0,1:T(8,128)(2,1)S(1)}, bf16[256,512]{0,1:T(8,128)(2,1)S(1)}, u32[]{:S(2)}, u32[]{:S(2)}) collective-permute-start(bf16[256,512]{0,1:T(8,128)(2,1)S(1)} %slice.454), channel_id=1, source_target_pairs={{0,4},{4,0},{8,12},{12,8},{16,20},{20,16},{24,28},{28,24},{32,36},... | collective-permute-start | bytes 786440 | tf_op jit(solution)/shard_map/ppermute | solution.py:17
  189.9 3.4 collective-permute-start.1
  193.5 0.9 copy-start.2
  197.5 352.6 %copy-start.3 = (bf16[256,1536]{0,1:T(8,128)(2,1)S(1)}, bf16[256,1536]{0,1:T(8,128)(2,1)}, u32[]{:S(2)}) copy-start(bf16[256,1536]{0,1:T(8,128)(2,1)} %copy-done.2) | copy-start | bytes 2359300
  197.5 463.1 %all-reduce.5.cloned.1.call-start = ((), (), s32[]{:S(2)}) async-start(), calls=%async_computation.3 | async-start | bytes 8388608 | tf_op jit(solution)/shard_map/psum | solution.py:119
  552.3 48.2 %all-to-all-start.1 = ((bf16[128,2,1024]{2,1,0:T(2,128)(2,1)}), bf16[128,2,1024]{2,1,0:T(2,128)(2,1)S(1)}, u32[]{:S(2)}, u32[]{:S(2)}) async-start(bf16[128,2,1024]{2,1,0:T(2,128)(2,1)} %reshape.123), calls=%async_computation.1 | async-start | bytes 1048576 | tf_op jit(solution)/shard_map/all_to_all | solution.py:21
Sparse Core Ops, SparseCore 0:
  11.1 147.9 all-gather.3
  197.6 352.4 all-reduce.2
  552.6 107.9 all-reduce.4
